TPU v7x, 32 devices: a whole 2x2x4 slice. The times are simulated.
32 devices in a mesh: parts: 2 (over x), space: 16 (over z, y, core).
Axes of the slice: x: 2, y: 2, z: 4, core: 2. Of those that a mesh axis runs over, the one named last changes fastest.
Arguments:
- images: bfloat16 [8, 32, 128, 512], P('parts', 'space'), parts along dimension 0, may hold values from 0 to 0.099609375
- target: bfloat16 [8, 16, 64, 1024], P('parts', 'space'), parts along dimension 0, may hold values from -8 to 8
- raw_filters: bfloat16 [2048, 3, 3, 512], P(('parts', 'space')), parts along dimension 0, may hold values from -39 to 39
Outputs:
- input_grads: bfloat16 [8, 32, 128, 512], P('parts', 'space'), parts along dimension 0
- filter_grads: float32 [2048, 3, 3, 512], P(('parts', 'space')), parts along dimension 0
There are 2 independent parts, one for each index of `parts`. A program takes and returns all parts, laid end to end along the dimension named above; each array names one. Nothing has to cross between parts.
All inputs are finite; a program needn't handle non-finite values.
Results may differ from a plain program's by a relative error of at most 0.008.
Values may be sent and summed in bfloat16 or wider, within the bound.
A program may use at most 128 MiB of HBM per device.

v0:
```python
import jax
import jax.numpy as jnp
from jax import lax
from jax.sharding import PartitionSpec as P

EPS = 1e-05
GRAD_SCALE = 0.015625


def passed_along(block, axis, distance):
    devices = range(lax.axis_size(axis))
    route = [(i - distance, i) for i in devices if i - distance in devices]
    return lax.ppermute(block, axis, route)


def standardize(rows):
    values = rows.astype(jnp.float32)
    centre = jnp.mean(values, axis=1, keepdims=True)
    shifted = values - centre
    spread = jnp.sqrt(jnp.mean(shifted * shifted, axis=1, keepdims=True) + EPS)
    return (shifted / spread, spread)


def place_row(taps):
    count_img, out_cols, three, channels = taps.shape
    evens = taps[:, :, 1]
    later = jnp.concatenate([taps[:, 1:, 0], jnp.zeros_like(taps[:, :1, 0])], axis=1)
    odds = taps[:, :, 2] + later
    return jnp.stack([evens, odds], axis=2).reshape(count_img, 2 * out_cols, channels)


def shards(images, target, raw_filters):
    count_img, two_rows, in_cols, cin = images.shape
    out_cols = in_cols // 2
    own_count = raw_filters.shape[0]
    cout_total = own_count * lax.axis_size("space")
    pixels = count_img * out_cols
    fan = 9 * cin
    rim = passed_along(images[:, 1:2], "space", 1)
    three_rows = jnp.concatenate([rim, images], axis=1)
    padded = jnp.pad(three_rows, ((0, 0), (0, 0), (1, 1), (0, 0)))
    tap_list = []
    for kh in range(3):
        for kw in range(3):
            tap_list.append(padded[:, kh, kw : kw + 2 * out_cols : 2, :])
    patches = jnp.concatenate(tap_list, axis=-1).reshape(pixels, fan)
    wanted = target.reshape(pixels, cout_total)
    own_rows = raw_filters.reshape(own_count, fan)
    first_tap = 0
    own_hat, own_spread = standardize(own_rows)
    sent_rows = own_hat.astype(jnp.bfloat16)
    rows_bf = lax.all_gather(sent_rows, "space", axis=0, tiled=True)
    block = lax.dot_general(
        patches, rows_bf, (((1,), (1,)), ((), ())), preferred_element_type=jnp.float32
    )
    goal = wanted.astype(jnp.float32)
    grad_block = ((block - goal) * GRAD_SCALE).astype(jnp.bfloat16)
    columns = jnp.dot(grad_block, rows_bf, preferred_element_type=jnp.float32)
    top_rows = rows_bf[:, :first_tap]
    state = (columns, grad_block, top_rows)
    columns, grad_all, top_rows = state
    summed = lax.psum_scatter(
        lax.dot_general(
            grad_all, patches, (((0,), (0,)), ((), ())), preferred_element_type=jnp.float32
        ),
        "space",
        scatter_dimension=0,
        tiled=True,
    )
    first_mean = jnp.mean(summed, axis=1, keepdims=True)
    second_mean = jnp.mean(summed * own_hat, axis=1, keepdims=True)
    filter_grads = ((summed - first_mean - own_hat * second_mean) / own_spread).reshape(
        raw_filters.shape
    )
    grid = columns.reshape(count_img, out_cols, 3, 3, cin)
    upper = place_row(grid[:, :, 0])
    middle = place_row(grid[:, :, 1])
    lower = place_row(grid[:, :, 2])
    from_below = passed_along(upper.astype(jnp.bfloat16), "space", -1).astype(upper.dtype)
    input_grads = jnp.stack([middle, lower + from_below], axis=1).astype(jnp.bfloat16)
    return (input_grads, filter_grads)


def solution(mesh):
    return jax.shard_map(
        shards,
        mesh=mesh,
        in_specs=(
            P("parts", "space", None, None),
            P("parts", "space", None, None),
            P(("parts", "space"), None, None, None),
        ),
        out_specs=(P("parts", "space", None, None), P(("parts", "space"), None, None, None)),
        check_vma=False,
    )
```

profile of v0, /device:TPU:0, one launch (start us, length us, event | category | flops | bytes accessed | tf_op | source)
XLA Modules:
  0.0 317.3 jit_solution(565481155447726842)
XLA Ops:
  7.2 1.3 convert_reduce_fusion
  8.5 1.6 copy.21
  11.4 1.0 fusion.12
  12.9 2.4 collective-permute-start
  15.3 1.5 collective-permute-done
  16.8 1.6 fusion.3
  18.4 2.6 slice.76
  21.1 2.6 slice.75
  23.7 2.7 slice.74
  26.3 2.6 slice.73
  29.0 2.6 slice.72
  31.6 2.7 slice.71
  34.2 2.6 slice.70
  36.8 2.6 slice.69
  39.5 2.7 slice.77
  42.1 1.0 constant_dynamic-update-slice_fusion.8
  44.1 1.0 constant_dynamic-update-slice_fusion.6
  45.1 1.0 constant_dynamic-update-slice_fusion.5
  50.0 46.2 %all-gather.2.cloned.1.call-done = bf16[1024,4608]{1,0:T(8,128)(2,1)} async-done(((bf16[64,4608]{1,0:T(8,128)(2,1)}), bf16[1024,4608]{1,0:T(8,128)(2,1)}) %all-gather.2.cloned.1.call-update) | async-done | bytes 9437200 | tf_op jit(solution)/shard_map/all_gather | solution.py:52
  96.2 6.5 %fusion.5 = bf16[256,1024]{1,0:T(8,128)(2,1)S(1)} fusion(bf16[256,4608]{1,0:T(8,128)(2,1)S(1)} %constant_dynamic-update-slice_fusion, bf16[1024,4608]{1,0:T(8,128)(2,1)} %all-gather.2.cloned.1.call-done, bf16[256,1024]{1,0:T(8,128)(2,1)} %bitcast.76), kind=kOutput, calls=%fused_computation.11 | convolution fusion | flops 2416967680 | bytes 12845056 | tf_op jit(solution)/shard_map/dot_general | solution.py:53
  103.5 7.9 %fusion.16 = f32[1024,4608]{1,0:T(8,128)} fusion(bf16[256,1024]{1,0:T(8,128)(2,1)S(1)} %fusion.5, bf16[256,4608]{1,0:T(8,128)(2,1)S(1)} %constant_dynamic-update-slice_fusion), kind=kOutput, calls=%fused_computation.53 | convolution fusion | flops 2415919104 | bytes 21757952 | tf_op jit(solution)/shard_map/dot_general | solution.py:63
  111.5 1.0 copy-done.3
  112.5 8.6 %fusion.15 = f32[256,4608]{1,0:T(8,128)} fusion(bf16[256,1024]{1,0:T(8,128)(2,1)S(1)} %copy-done.3, bf16[1024,4608]{1,0:T(8,128)(2,1)} %all-gather.2.cloned.1.call-done), kind=kOutput, calls=%fused_computation.52 | convolution fusion | flops 2415919104 | bytes 14680064 | tf_op jit(solution)/shard_map/dot_general | solution.py:58
  121.1 9.1 %reshape.65 = f32[4,64,3,3,512]{4,3,2,1,0:T(4,128)} reshape(f32[256,4608]{1,0:T(8,128)} %fusion.15) | data formatting | bytes 9437184 | tf_op jit(solution)/shard_map/reshape | solution.py:75
  130.2 5.4 %slice_bitcast_fusion.2 = (f32[4,64,3,512]{3,2,1,0:T(4,128)S(1)}, f32[4,64,3,512]{3,2,1,0:T(4,128)S(1)}, f32[4,64,3,512]{3,2,1,0:T(4,128)S(1)}) fusion(f32[4,64,3,3,512]{4,3,2,1,0:T(4,128)} %reshape.65), kind=kLoop, calls=%fused_computation.7 | loop fusion | bytes 9437184 | tf_op jit(solution)/shard_map/squeeze | solution.py:77
  138.2 1.5 collective-permute-start.1
  144.8 1.2 copy.28
  146.0 158.1 %reduce-scatter.2.cloned.1.call-done = f32[64,4608]{1,0:T(8,128)} async-done(((f32[1024,4608]{1,0:T(8,128)}), f32[64,4608]{1,0:T(8,128)}) %reduce-scatter.2.cloned.1.call-update) | async-done | bytes 1179664 | tf_op jit(solution)/shard_map/reduce_scatter | solution.py:62
  304.1 1.7 fusion.13
  305.8 1.3 subtract_divide_fusion
  307.1 1.9 reshape.67
  309.1 1.4 copy.29
  (53 shorter events, 14.9 us)
Async XLA Ops:
  7.2 3.0 copy-start
  7.2 89.0 %all-gather.2.cloned.1.call-start = ((), (), s32[]{:S(2)}) async-start(), calls=%async_computation.1 | async-start | bytes 10027008 | tf_op jit(solution)/shard_map/all_gather | solution.py:52
  11.4 1.4 copy-start.4
  12.4 291.6 %reduce-scatter.2.cloned.1.call-start = ((), (), s32[]{:S(2)}) async-start(), calls=%async_computation.2 | async-start | bytes 20054016 | tf_op jit(solution)/shard_map/reduce_scatter | solution.py:62
  12.9 3.9 %collective-permute-start = (bf16[4,1,128,512]{3,2,1,0:T(8,128)(2,1)S(1)}, bf16[4,1,128,512]{3,2,1,0:T(8,128)(2,1)S(1)}, u32[]{:S(2)}, u32[]{:S(2)}) collective-permute-start(bf16[4,1,128,512]{3,2,1,0:T(8,128)(2,1)S(1)} %slice.68), channel_id=1, source_target_pairs={{0,1},{1,2},{2,3},{3,4},{4,5},{5,6},{6,7},{7,8},{8,9},{9,10},{10,1... | collective-permute-start | bytes 1572872 | tf_op jit(solution)/shard_map/ppermute | solution.py:13
  42.1 7.8 %copy-start.5 = (bf16[4,1,64,512]{3,2,1,0:T(8,128)(2,1)S(1)}, bf16[4,1,64,512]{3,2,1,0:T(8,128)(2,1)}, u32[]{:S(2)}) copy-start(bf16[4,1,64,512]{3,2,1,0:T(8,128)(2,1)} %slice.77) | copy-start | bytes 786436
  102.7 0.8 copy-start.2
  111.4 1.0 copy-start.3
  138.2 5.5 %collective-permute-start.1 = (bf16[4,128,512]{2,0,1:T(4,128)(2,1)S(1)}, bf16[4,128,512]{2,0,1:T(4,128)(2,1)S(1)}, u32[]{:S(2)}, u32[]{:S(2)}) collective-permute-start(bf16[4,128,512]{2,0,1:T(4,128)(2,1)S(1)} %bitcast.75), channel_id=1, source_target_pairs={{1,0},{2,1},{3,2},{4,3},{5,4},{6,5},{7,6},{8,7},{9,8},{10,9},{11,1... | collective-permute-start | bytes 1572872 | tf_op jit(solution)/shard_map/ppermute | solution.py:13
  304.1 1.7 copy-start.1
Sparse Core Ops, SparseCore 0:
  12.5 83.6 all-gather.1
  111.6 192.4 reduce-scatter.1
where the time goes:
time: 318 us; the launch traced here: 317 us
  waiting for transfers between devices  206 us (65%)
  local copies, waits for them, and re-layouts  61.2 us (19%)
  matrix products  23 us (7%)
  between operations  14.4 us (5%)
  other arithmetic  8.92 us (3%)
  starting transfers between devices  3.98 us (1%)
    reduce_scatter x1, waiting for transfers between devices, shards(): lax.psum_scatter(lax.dot_general(grad_all, patches, (((0,), (0,)), ((), (...  158 us
    all_gather x1, waiting for transfers between devices, shards(): rows_bf = lax.all_gather(sent_rows, 'space', axis=0, tiled=True)  46.2 us
    slice x9, local copies, waits for them, and re-layouts, shards(): tap_list.append(padded[:, kh, kw:kw + 2 * out_cols:2, :])  23.7 us
    unnamed x28, local copies, waits for them, and re-layouts  12.7 us
    reshape x1, local copies, waits for them, and re-layouts, shards(): grid = columns.reshape(count_img, out_cols, 3, 3, cin)  9.11 us
    dot_general x1, matrix products, shards(): columns = jnp.dot(grad_block, rows_bf, preferred_element_type=jnp.float32)  8.63 us
    dot_general x1, matrix products, shards(): lax.dot_general(grad_all, patches, (((0,), (0,)), ((), ())), preferred_el...  7.93 us
    dot_general x1, matrix products, shards(): lax.dot_general(patches, rows_bf, (((1,), (1,)), ((), ())), preferred_ele...  6.48 us
  transfers between devices with their start and end apart: 4, of which 3 were waited for; matrix products, arithmetic and copies ran while one was open for 20% of the time, Pallas kernels for 0%

commit v1 on v0

v1 whole, which is shorter than its diff:
```python
import jax
import jax.numpy as jnp
from jax import lax
from jax.sharding import PartitionSpec as P

EPS = 1e-05
GRAD_SCALE = 0.015625
GROUP = 4


def standardize(rows):
    values = rows.astype(jnp.float32)
    centre = jnp.mean(values, axis=1, keepdims=True)
    shifted = values - centre
    spread = jnp.sqrt(jnp.mean(shifted * shifted, axis=1, keepdims=True) + EPS)
    return (shifted / spread, spread)


def dot(a, b, dims):
    return lax.dot_general(a, b, (dims, ((), ())), preferred_element_type=jnp.float32)


def shards(images, target, raw_filters):
    count_img, two_rows, in_cols, cin = images.shape
    half = in_cols // 2
    own_count = raw_filters.shape[0]
    devices = lax.axis_size("space")
    wide = GROUP if devices % GROUP == 0 else 1
    tall = devices // wide
    near = [[r * wide + f for f in range(wide)] for r in range(tall)]
    far = [[r * wide + f for r in range(tall)] for f in range(wide)]
    fan = 9 * cin
    bf = jnp.bfloat16
    pair = images.reshape(count_img, two_rows, half, 2 * cin)
    own_hat, own_spread = standardize(raw_filters.reshape(own_count, fan))
    rows_bf = lax.all_gather(own_hat.astype(bf), "space", axis_index_groups=far, tiled=True)
    tiles = lax.all_gather(pair, "space", axis_index_groups=near)
    wanted = target.reshape(count_img, half, tall, wide, own_count)
    wanted = lax.all_to_all(
        wanted, "space", 3, 0, axis_index_groups=near, tiled=False
    )
    wanted = wanted.reshape(wide, count_img * half, tall * own_count)
    route = [(i, i + wide) for i in range(devices - wide)]
    last = lax.ppermute(tiles[-1, :, 1], "space", route)
    filters = tall * own_count
    rows = jnp.concatenate(
        [last[None, :], tiles.transpose(0, 2, 1, 3, 4).reshape(2 * wide, count_img, half, 2 * cin)],
        axis=0,
    )
    odd = rows[..., cin:]
    before = jnp.pad(odd[:, :, :-1], ((0, 0), (0, 0), (1, 0), (0, 0)))
    full = jnp.concatenate([before, rows], axis=-1).reshape(2 * wide + 1, count_img * half, 3 * cin)
    patches = jnp.concatenate([full[k : k + 2 * wide : 2] for k in range(3)], axis=-1)
    patches = patches.reshape(wide * count_img * half, fan)
    block = dot(patches, rows_bf, ((1,), (1,)))
    goal = wanted.reshape(wide * count_img * half, filters).astype(jnp.float32)
    grad = ((block - goal) * GRAD_SCALE).astype(bf)
    part = dot(grad, patches, ((0,), (0,)))
    summed = lax.psum_scatter(
        part.astype(bf), "space", axis_index_groups=far, tiled=True
    ).astype(jnp.float32)
    columns = dot(grad, rows_bf, ((1,), (0,))).reshape(wide, count_img, half, 3, 3, cin)
    later = jnp.pad(columns[:, :, 1:, :, 0], ((0, 0), (0, 0), (0, 1), (0, 0), (0, 0)))
    odds = columns[:, :, :, :, 2] + later
    both = jnp.concatenate([columns[:, :, :, :, 1], odds], axis=-1)
    upper, middle, lower = both[:, :, :, 0], both[:, :, :, 1], both[:, :, :, 2]
    lower = lower + jnp.concatenate([upper[1:], jnp.zeros_like(upper[:1])], axis=0)
    inner = jnp.stack([middle, lower], axis=1).astype(bf)
    mine = lax.psum_scatter(inner, "space", axis_index_groups=near, tiled=False)
    back = [(i + wide, i) for i in range(devices - wide)]
    edge = lax.ppermute(upper[0].astype(bf), "space", back)
    edge = lax.psum_scatter(
        jnp.stack([jnp.zeros_like(edge)] * (wide - 1) + [edge]), "space", axis_index_groups=near, tiled=False
    )
    low = (mine[1].astype(jnp.float32) + edge.astype(jnp.float32)).astype(bf)
    input_grads = jnp.stack([mine[0], low], axis=1).reshape(images.shape)
    first_mean = jnp.mean(summed, axis=1, keepdims=True)
    second_mean = jnp.mean(summed * own_hat, axis=1, keepdims=True)
    filter_grads = ((summed - first_mean - own_hat * second_mean) / own_spread).reshape(
        raw_filters.shape
    )
    return (input_grads, filter_grads)


def solution(mesh):
    return jax.shard_map(
        shards,
        mesh=mesh,
        in_specs=(
            P("parts", "space", None, None),
            P("parts", "space", None, None),
            P(("parts", "space"), None, None, None),
        ),
        out_specs=(P("parts", "space", None, None), P(("parts", "space"), None, None, None)),
        check_vma=False,
    )
```

time: 318 us -> 387 us (1.22)
  local copies, waits for them, and re-layouts: 61.2 us -> 95.2 us
  other arithmetic: 8.92 us -> 30.2 us
  waiting for transfers between devices: 206 us -> 213 us
  starting transfers between devices: 3.98 us -> 9.94 us
    reduce_scatter x1 -> x2, waiting for transfers between devices: 158 us -> 74.5 us  [the longest x1 46.7 us: shards(): lax.psum_scatter(part.astype(bf), 'space', axis_index_groups=far, tiled=T...]
    unnamed x2 -> x6, waiting for transfers between devices: 0.03 us -> 58.9 us
    ppermute x2, waiting for transfers between devices: 1.49 us -> 28.2 us  [the longest x1 15.3 us: shards(): edge = lax.ppermute(upper[0].astype(bf), 'space', back)]
    reshape x1, local copies, waits for them, and re-layouts: 9.11 us -> 30.4 us  [shards(): dot(grad, rows_bf, ((1,), (0,))).reshape(wide, count_img, half, 3, 3, cin)]
    slice x18 -> x5, local copies, waits for them, and re-layouts: 27.9 us -> 40 us  [the longest x2 27.5 us: shards(): both = jnp.concatenate([columns[:, :, :, :, 1], odds], axis=-1)]
    add x0 -> x1, other arithmetic: none -> 7.04 us  [shards(): odds = columns[:, :, :, :, 2] + later]
    concatenate x1 -> x3, other arithmetic: 1.65 us -> 8.53 us  [the longest x1 3.97 us: shards(): jnp.concatenate([full[k:k + 2 * wide:2] for k in range(3)], axis=-1)]
    unnamed x28 -> x26, local copies, waits for them, and re-layouts: 12.7 us -> 6.74 us
  transfers between devices with their start and end apart: 4 -> 8, of which waited for: 3 -> 7; matrix products, arithmetic and copies ran while one was open for 20% -> 12% of each run, Pallas kernels for 0% -> 0%
where the time goes in v1:
time: 387 us; the launch traced here: 385 us
  waiting for transfers between devices  213 us (55%)
  local copies, waits for them, and re-layouts  95.2 us (25%)
  other arithmetic  30.2 us (8%)
  matrix products  22.7 us (6%)
  between operations  14.1 us (4%)
  starting transfers between devices  9.94 us (3%)
    unnamed x6, waiting for transfers between devices  58.9 us
    reduce_scatter x1, waiting for transfers between devices, shards(): lax.psum_scatter(part.astype(bf), 'space', axis_index_groups=far, tiled=T...  46.7 us
    reshape x1, local copies, waits for them, and re-layouts, shards(): dot(grad, rows_bf, ((1,), (0,))).reshape(wide, count_img, half, 3, 3, cin)  30.4 us
    all_gather x1, waiting for transfers between devices, shards(): tiles = lax.all_gather(pair, 'space', axis_index_groups=near)  30.4 us
    reduce_scatter x1, waiting for transfers between devices, shards(): lax.psum_scatter(jnp.stack([jnp.zeros_like(edge)] * (wide - 1) + [edge]),...  27.8 us
    slice x2, local copies, waits for them, and re-layouts, shards(): both = jnp.concatenate([columns[:, :, :, :, 1], odds], axis=-1)  27.5 us
    dot_general x3, matrix products, dot(): lax.dot_general(a, b, (dims, ((), ())), preferred_element_type=jnp.float32)  22.7 us
    all_gather x1, waiting for transfers between devices, shards(): lax.all_gather(own_hat.astype(bf), 'space', axis_index_groups=far, tiled=...  20.9 us
  transfers between devices with their start and end apart: 8, of which 7 were waited for; matrix products, arithmetic and copies ran while one was open for 12% of the time, Pallas kernels for 0%

profile of v1, /device:TPU:0, one launch (start us, length us, event | category | flops | bytes accessed | tf_op | source)
XLA Modules:
  0.0 385.0 jit_solution(16695776634072249279)
XLA Ops:
  7.2 2.2 all_gather_reshape.3
  9.5 1.6 copy.59
  13.7 2.5 broadcast_in_dim_reshape.3
  16.7 1.6 reshape.110
  18.3 4.3 %all-to-all-start = ((bf16[4,2,32768]{2,1,0:T(2,128)(2,1)}), bf16[4,2,32768]{2,1,0:T(2,128)(2,1)S(1)}, u32[]{:S(2)}, u32[]{:S(2)}) async-start(bf16[4,2,32768]{2,1,0:T(2,128)(2,1)} %reshape.110), calls=%async_computation | async-start | bytes 1048576 | tf_op jit(solution)/shard_map/all_to_all | solution.py:39
  22.6 30.4 %all-gather.3.cloned.1.call-done = bf16[4,4,2,64,1024]{4,3,2,1,0:T(8,128)(2,1)} async-done(((bf16[1,4,2,64,1024]{4,3,2,1,0:T(8,128)(2,1)}), bf16[4,4,2,64,1024]{4,3,2,1,0:T(8,128)(2,1)}) %all-gather.3.cloned.1.call-update) | async-done | bytes 4194320 | tf_op jit(solution)/shard_map/all_gather | solution.py:37
  53.0 1.9 slice_bitcast_fusion.3
  54.8 4.2 %collective-permute-start = (bf16[4,64,1024]{2,1,0:T(8,128)(2,1)}, bf16[4,64,1024]{2,1,0:T(8,128)(2,1)}, u32[]{:S(2)}, u32[]{:S(2)}) collective-permute-start(bf16[4,64,1024]{2,1,0:T(8,128)(2,1)} %slice_bitcast_fusion.3), channel_id=1, source_target_pairs={{0,4},{1,5},{2,6},{3,7},{4,8},{5,9},{6,10},{7,11},{8,12},{9,13},{1... | collective-permute-start | bytes 1572872 | tf_op jit(solution)/shard_map/ppermute | solution.py:44
  60.0 2.1 reshape.102
  62.1 2.9 copy.57
  65.0 12.9 %collective-permute-done = bf16[4,64,1024]{2,1,0:T(8,128)(2,1)} collective-permute-done((bf16[4,64,1024]{2,1,0:T(8,128)(2,1)}, bf16[4,64,1024]{2,1,0:T(8,128)(2,1)}, u32[]{:S(2)}, u32[]{:S(2)}) %collective-permute-start) | collective-permute-done | bytes 524320 | tf_op jit(solution)/shard_map/ppermute | solution.py:44
  77.9 2.3 fusion.6
  80.2 2.3 maximum_maximum_fusion
  83.6 4.0 %pad_maximum_fusion.1 = bf16[4,256,4608]{2,1,0:T(8,128)(2,1)} fusion(bf16[4,256,1536]{2,1,0:T(8,128)(2,1)S(1)} %get-tuple-element.19, bf16[4,256,1536]{2,1,0:T(8,128)(2,1)S(1)} %get-tuple-element.20, bf16[4,256,1536]{2,1,0:T(8,128)(2,1)S(1)} %get-tuple-element.18), kind=kLoop, calls=%fused_computation.3 | loop fusion | flops 28311552 | bytes 18874368 | tf_op jit(solution)/shard_map/concatenate | solution.py:53
  87.5 20.9 %all-gather.5.cloned.1.call-done = bf16[256,4608]{1,0:T(8,128)(2,1)} async-done(((bf16[64,4608]{1,0:T(8,128)(2,1)}), bf16[256,4608]{1,0:T(8,128)(2,1)}) %all-gather.5.cloned.1.call-update) | async-done | bytes 2359312 | tf_op jit(solution)/shard_map/all_gather | solution.py:36
  108.4 7.1 %fusion.9 = bf16[1024,256]{1,0:T(8,128)(2,1)S(1)} fusion(f32[1024,256]{1,0:T(8,128)S(1)} %copy-done.7, bf16[1024,4608]{1,0:T(8,128)(2,1)} %bitcast.82, bf16[256,4608]{1,0:T(8,128)(2,1)} %all-gather.5.cloned.1.call-done), kind=kOutput, calls=%fused_computation.28 | convolution fusion | flops 2416705536 | bytes 13369344 | tf_op jit(solution)/shard_map/dot_general | solution.py:20
  115.6 7.9 %fusion.17 = f32[1024,4608]{1,0:T(8,128)} fusion(bf16[1024,256]{1,0:T(8,128)(2,1)S(1)} %fusion.9, bf16[256,4608]{1,0:T(8,128)(2,1)S(1)} %copy-done.6), kind=kOutput, calls=%fused_computation.52 | convolution fusion | flops 2415919104 | bytes 21757952 | tf_op jit(solution)/shard_map/dot_general | solution.py:20
  123.5 30.4 %reshape.99 = f32[4,4,64,3,3,512]{5,4,3,2,1,0:T(4,128)} reshape(f32[1024,4608]{1,0:T(8,128)} %fusion.17) | data formatting | bytes 37748736 | tf_op jit(solution)/shard_map/reshape | solution.py:62
  153.9 26.4 %fusion.15 = (f32[4,4,64,3,1,512]{5,4,3,2,1,0:T(1,128)}, f32[4,4,64,3,1,512]{5,4,3,2,1,0:T(1,128)}) fusion(f32[4,4,64,3,3,512]{5,4,3,2,1,0:T(4,128)} %reshape.99), kind=kLoop, calls=%fused_computation.49 | loop fusion | bytes 25165824 | tf_op jit(solution)/shard_map/slice | solution.py:65
  180.4 10.3 %slice.73 = f32[4,4,63,3,1,512]{5,4,3,2,1,0:T(1,128)S(1)} slice(f32[4,4,64,3,3,512]{5,4,3,2,1,0:T(4,128)} %reshape.99), slice={[0:4], [0:4], [1:64], [0:3], [0:1], [0:512]} | slice | bytes 12386304 | tf_op jit(solution)/shard_map/slice | solution.py:63
  193.4 7.0 %bitcast_add_fusion = f32[4,4,64,3,512]{4,2,3,1,0:T(8,128)S(1)} fusion(f32[4,4,64,3,1,512]{5,4,3,2,1,0:T(1,128)} %get-tuple-element.17, f32[4,4,63,3,512]{4,2,3,1,0:T(8,128)S(1)} %bitcast.89), kind=kLoop, calls=%fused_computation.6 | loop fusion | flops 1572864 | bytes 18776064 | tf_op jit(solution)/shard_map/add | solution.py:64
  201.1 2.0 copy-done.1
  204.0 2.3 pad_maximum_fusion.2
  206.4 7.6 %convolution_convert_fusion = bf16[256,4608]{1,0:T(8,128)(2,1)} fusion(bf16[1024,256]{1,0:T(8,128)(2,1)S(1)} %fusion.9, bf16[1024,4608]{1,0:T(8,128)(2,1)} %bitcast.83), kind=kOutput, calls=%fused_computation.5 | convolution fusion | flops 2417098752 | bytes 12320768 | tf_op jit(solution)/shard_map/dot_general | solution.py:20
  216.8 15.3 %collective-permute-done.1 = bf16[4,64,1024]{2,1,0:T(8,128)(2,1)S(1)} collective-permute-done((bf16[4,64,1024]{2,1,0:T(8,128)(2,1)S(1)}, bf16[4,64,1024]{2,1,0:T(8,128)(2,1)S(1)}, u32[]{:S(2)}, u32[]{:S(2)}) %collective-permute-start.1) | collective-permute-done | bytes 524320 | tf_op jit(solution)/shard_map/ppermute | solution.py:71
  232.1 1.5 pad_maximum_fusion.3
  234.2 58.8 %all-reduce.6.cloned.1.call-done = bf16[4,2,4,64,1024]{4,3,2,0,1:T(8,128)(2,1)} async-done(((bf16[4,2,4,64,1024]{4,3,2,0,1:T(8,128)(2,1)}), bf16[4,2,4,64,1024]{4,3,2,0,1:T(8,128)(2,1)}) %all-reduce.6.cloned.1.call-update) | async-done | bytes 4194320
  293.0 2.0 constant_dynamic-slice_fusion
  296.3 46.7 %reduce-scatter.8.cloned.1.call-done = bf16[64,4608]{1,0:T(8,128)(2,1)} async-done(((bf16[256,4608]{1,0:T(8,128)(2,1)}), bf16[64,4608]{1,0:T(8,128)(2,1)}) %reduce-scatter.8.cloned.1.call-update) | async-done | bytes 589840 | tf_op jit(solution)/shard_map/reduce_scatter | solution.py:59
  343.0 1.5 convert_reduce_fusion
  344.5 1.4 fusion.11
  348.2 27.8 %reduce-scatter.6.cloned.1.call-done = bf16[1,4,64,1024]{3,2,1,0:T(8,128)(2,1)} async-done(((bf16[4,4,64,1024]{3,2,1,0:T(8,128)(2,1)}), bf16[1,4,64,1024]{3,2,1,0:T(8,128)(2,1)}) %reduce-scatter.6.cloned.1.call-update) | async-done | bytes 524304 | tf_op jit(solution)/shard_map/reduce_scatter | solution.py:72
  (61 shorter events, 18.8 us)
Async XLA Ops:
  7.2 4.9 %copy-start.4 = (bf16[64,3,3,512]{3,0,2,1:T(8,128)(2,1)S(1)}, bf16[64,3,3,512]{3,0,2,1:T(8,128)(2,1)}, u32[]{:S(2)}) copy-start(bf16[64,3,3,512]{3,0,2,1:T(8,128)(2,1)} %param.5) | copy-start | bytes 1769476
  7.2 45.8 %all-gather.3.cloned.1.call-start = ((), (), s32[]{:S(2)}) async-start(), calls=%async_computation.3 | async-start | bytes 5242880 | tf_op jit(solution)/shard_map/all_gather | solution.py:37
  9.5 98.9 %all-gather.5.cloned.1.call-start = ((), (), s32[]{:S(2)}) async-start(), calls=%async_computation.4 | async-start | bytes 2949120 | tf_op jit(solution)/shard_map/all_gather | solution.py:36
  12.1 6.2 %copy-start.2 = (f32[64,4608]{1,0:T(8,128)}, f32[64,4608]{1,0:T(8,128)S(1)}, u32[]{:S(2)}) copy-start(f32[64,4608]{1,0:T(8,128)S(1)} %reshape.101) | copy-start | bytes 3538948
  18.3 40.7 %all-to-all-start = ((bf16[4,2,32768]{2,1,0:T(2,128)(2,1)}), bf16[4,2,32768]{2,1,0:T(2,128)(2,1)S(1)}, u32[]{:S(2)}, u32[]{:S(2)}) async-start(bf16[4,2,32768]{2,1,0:T(2,128)(2,1)} %reshape.110), calls=%async_computation | async-start | bytes 1048576 | tf_op jit(solution)/shard_map/all_to_all | solution.py:39
  22.6 270.4 %all-reduce.6.cloned.1.call-start = ((), (), s32[]{:S(2)}) async-start(), calls=%async_computation.7 | async-start | bytes 8388608
  54.8 23.1 %collective-permute-start = (bf16[4,64,1024]{2,1,0:T(8,128)(2,1)}, bf16[4,64,1024]{2,1,0:T(8,128)(2,1)}, u32[]{:S(2)}, u32[]{:S(2)}) collective-permute-start(bf16[4,64,1024]{2,1,0:T(8,128)(2,1)} %slice_bitcast_fusion.3), channel_id=1, source_target_pairs={{0,4},{1,5},{2,6},{3,7},{4,8},{5,9},{6,10},{7,11},{8,12},{9,13},{1... | collective-permute-start | bytes 1572872 | tf_op jit(solution)/shard_map/ppermute | solution.py:44
  83.5 24.9 %copy-start.7 = (f32[1024,256]{1,0:T(8,128)S(1)}, f32[1024,256]{1,0:T(8,128)}, u32[]{:S(2)}) copy-start(f32[1024,256]{1,0:T(8,128)} %reshape.102) | copy-start | bytes 3145732
  108.4 7.1 %copy-start.6 = (bf16[256,4608]{1,0:T(8,128)(2,1)S(1)}, bf16[256,4608]{1,0:T(8,128)(2,1)}, u32[]{:S(2)}) copy-start(bf16[256,4608]{1,0:T(8,128)(2,1)} %all-gather.5.cloned.1.call-done) | copy-start | bytes 7077892
  180.4 11.4 %slice-start = ((s8[6291456]{0:T(1024)(128)(4,1)}), s8[4194304]{0:T(1024)(128)(4,1)S(1)}, s32[]{:S(2)}) async-start(s8[6291456]{0:T(1024)(128)(4,1)} %bitcast.87), calls=%async_computation.8 | async-start | bytes 8388608
  190.7 1.6 slice-start.1
  193.4 7.7 %copy-start = (f32[4,4,64,3,1,512]{5,2,4,3,1,0:T(8,128)}, f32[4,4,64,3,1,512]{5,2,4,3,1,0:T(8,128)S(1)}, u32[]{:S(2)}) copy-start(f32[4,4,64,3,1,512]{5,2,4,3,1,0:T(8,128)S(1)} %copy.86) | copy-start | bytes 18874372
  200.4 2.6 copy-start.1
  206.3 136.7 %reduce-scatter.8.cloned.1.call-start = ((), (), s32[]{:S(2)}) async-start(), calls=%async_computation.6 | async-start | bytes 2949120 | tf_op jit(solution)/shard_map/reduce_scatter | solution.py:59
  214.0 162.0 %reduce-scatter.6.cloned.1.call-start = ((), (), s32[]{:S(2)}) async-start(), calls=%async_computation.5 | async-start | bytes 2621440 | tf_op jit(solution)/shard_map/reduce_scatter | solution.py:72
  215.3 18.3 %copy-start.8 = (u32[32]{0:T(128)S(1)}, u32[32]{0:T(128)}, u32[]{:S(2)}) copy-start(u32[32]{0:T(128)} %constant.29) | copy-start | bytes 388
  215.4 16.7 %collective-permute-start.1 = (bf16[4,64,1024]{2,1,0:T(8,128)(2,1)S(1)}, bf16[4,64,1024]{2,1,0:T(8,128)(2,1)S(1)}, u32[]{:S(2)}, u32[]{:S(2)}) collective-permute-start(bf16[4,64,1024]{2,1,0:T(8,128)(2,1)S(1)} %slice_bitcast_fusion.2), channel_id=1, source_target_pairs={{4,0},{5,1},{6,2},{7,3},{8,4},{9,5},{10,6},{11,7},{12,8},{13,9},{1... | collective-permute-start | bytes 1572872 | tf_op jit(solution)/shard_map/ppermute | solution.py:71
  233.6 109.5 %copy-start.3 = (f32[64,4608]{1,0:T(8,128)S(1)}, f32[64,4608]{1,0:T(8,128)}, u32[]{:S(2)}) copy-start(f32[64,4608]{1,0:T(8,128)} %copy-done.2) | copy-start | bytes 3538948
  346.8 30.3 %copy-start.5 = (f32[4,1,128,512]{3,2,0,1:T(8,128)S(1)}, f32[4,1,128,512]{3,2,0,1:T(8,128)}, u32[]{:S(2)}) copy-start(f32[4,1,128,512]{3,2,0,1:T(8,128)} %reshape.103) | copy-start | bytes 3145732
Sparse Core Ops, SparseCore 0:
  10.1 42.7 all-gather.2
  54.5 53.8 all-gather.4
  206.4 86.5 all-reduce.5
  295.2 47.8 reduce-scatter.7
  345.4 30.5 reduce-scatter.5

commit v2 on v0

v2 whole, which is shorter than its diff:
```python
import functools

import jax
import jax.numpy as jnp
from jax import lax
from jax.experimental import pallas as pl
from jax.experimental.pallas import tpu as pltpu
from jax.sharding import PartitionSpec as P

EPS = 1e-05
GRAD_SCALE = 0.015625
WIDE = 4
F32 = jnp.float32
BF = jnp.bfloat16
NT = (((1,), (1,)), ((), ()))
NN = (((1,), (0,)), ((), ()))


def standardize(rows):
    values = rows.astype(F32)
    centre = jnp.mean(values, axis=1, keepdims=True)
    shifted = values - centre
    spread = jnp.sqrt(jnp.mean(shifted * shifted, axis=1, keepdims=True) + EPS)
    return (shifted / spread, spread)


def dot(a, b, dims):
    return lax.dot_general(a, b, dims, preferred_element_type=F32)


def kernel(
    tall, own, half, cin,
    pair, goal, hat, dout, gout,
    x, w, tg, gy, gys, gt, gts, g,
    up_in, dn_in, up_out, dn_out,
    to_p, from_p, to_q, from_q, acc, rim_s, rim_p, rim_q, rim_z,
    x_recv, x_send, w_recv, w_up, w_dn, t_recv, t_send, r_recv, r_send,
    gu_recv, gu_send, gd_recv, gd_send, d_recv, d_send, e_recv, e_send,
):
    me = lax.axis_index("space")
    r, f = me // WIDE, me % WIDE
    base = r * WIDE
    fp = f + 1 - 2 * (f % 2)
    fq = f + 2 - 4 * (f // 2)
    fd = fp + 2 - 4 * (fp // 2)
    p, q, d = base + fp, base + fq, base + fd
    above, below = me - WIDE, me + WIDE
    px = pair.shape[1]
    two, one = 2 * cin, cin
    three = 3 * cin

    def rc(src, dst, ssem, rsem, to):
        return pltpu.make_async_remote_copy(
            src_ref=src, dst_ref=dst, send_sem=ssem, recv_sem=rsem,
            device_id={"space": to}, device_id_type=pl.DeviceIdType.MESH,
        )

    def wait_in(dst, rsem):
        rc(dst, dst, rsem, rsem, p).wait_recv()

    bar = pltpu.get_barrier_semaphore()

    def greet(to):
        pl.semaphore_signal(bar, inc=1, device_id={"space": to}, device_id_type=pl.DeviceIdType.MESH)

    for to in (p, q, d):
        greet(to)

    @pl.when(r > 0)
    def _():
        greet(above)

    @pl.when(r < tall - 1)
    def _():
        greet(below)

    inside = (r > 0) & (r < tall - 1)

    @pl.when(inside)
    def _():
        pl.semaphore_wait(bar, 5)

    @pl.when(jnp.logical_not(inside))
    def _():
        pl.semaphore_wait(bar, 4)

    def own_rows(b):
        return pl.ds(pl.multiple_of(b * own, own), own)

    def img_copy(row, k, to):
        slot = x.at[1 + 2 * f + row]
        return rc(pair.at[row], slot, x_send.at[k, row], x_recv.at[f, row], to)

    def fwd_copy(row):
        slot = x.at[1 + 2 * fq + row]
        return rc(slot, slot, x_send.at[2, row], x_recv.at[fq, row], p)

    def tgt_copy(k, to_f, to):
        return rc(goal.at[to_f], tg.at[f], t_send.at[k], t_recv.at[f], to)

    def w_copy(b, first, sem, to):
        slot = w.at[own_rows(b)]
        return rc(hat if first else slot, slot, sem.at[b], w_recv.at[b], to)

    rim_in = rc(pair.at[1], x.at[0], r_send.at[0], r_recv, below)
    rim_to_p = rc(x.at[0], x.at[0], r_send.at[1], r_recv, p)
    rim_to_q = rc(x.at[0], x.at[0], r_send.at[2], r_recv, q)

    def filters_step(s):
        b_up, b_dn = r - s, r + s

        @pl.when(b_up >= 0)
        def _():
            if s > 0:
                wait_in(w.at[own_rows(b_up)], w_recv.at[b_up])

            @pl.when(r < tall - 1)
            def _():
                w_copy(b_up, s == 0, w_up, below).start()

        @pl.when(b_dn <= tall - 1)
        def _():
            if s > 0:
                wait_in(w.at[own_rows(b_dn)], w_recv.at[b_dn])

            @pl.when(r > 0)
            def _():
                w_copy(b_dn, s == 0, w_dn, above).start()

    @pl.when((f == 3) & (r < tall - 1))
    def _():
        rim_in.start()

    filters_step(0)
    for row in range(2):
        img_copy(row, 1, q).start()
    for row in range(2):
        img_copy(row, 0, p).start()
    tgt_copy(0, fp, p).start()
    tgt_copy(1, fq, q).start()
    tgt_copy(2, fd, d).start()
    for row in range(2):
        x[1 + 2 * f + row] = pair[row]
    w[own_rows(r)] = hat[...]
    tg[f] = goal[f]

    def forward_row(row):
        wait_in(x.at[1 + 2 * fq + row], x_recv.at[fq, row])
        fwd_copy(row).start()

    def rim_step():
        @pl.when(r > 0)
        def _():
            wait_in(x.at[0], r_recv)

            @pl.when(f == 3)
            def _():
                rim_to_q.start()

            @pl.when(f % 2 == 1)
            def _():
                rim_to_p.start()

        @pl.when(r == 0)
        def _():
            x[0] = jnp.zeros((px, two), BF)

    for s in range(1, tall):
        filters_step(s)
        if s == 1:
            forward_row(0)
            rim_step()
        if s == 2:
            forward_row(1)
    for row in range(2):
        wait_in(x.at[1 + 2 * fp + row], x_recv.at[fp, row])
        wait_in(x.at[1 + 2 * fd + row], x_recv.at[fd, row])
    for t in (fp, fq, fd):
        wait_in(tg.at[t], t_recv.at[t])

    filters = tall * own
    place = lax.broadcasted_iota(jnp.int32, (px, filters), 0) % half
    gy[WIDE] = jnp.zeros((px, filters), BF)
    gys[WIDE] = jnp.zeros((px, filters), BF)

    def forward(t, carry):
        both = jnp.zeros((px, filters), F32)
        left = jnp.zeros((px, filters), F32)
        for kh in range(3):
            c = kh * three
            both += dot(x[2 * t + kh], w[:, c + one : c + three], NT)
            left += dot(x[2 * t + kh, :, one:two], w[:, c : c + one], NT)
        out = both + jnp.where(place == 0, 0.0, pltpu.roll(left, 1, 0))
        grad = ((out - tg[t].astype(F32)) * GRAD_SCALE).astype(BF)
        wide = grad.astype(F32)
        ahead = jnp.where(place == half - 1, 0.0, pltpu.roll(wide, px - 1, 0))
        gy[t] = grad
        gys[t] = ahead.astype(BF)
        gt[t] = wide.T.astype(BF)
        gts[t] = ahead.T.astype(BF)
        return carry

    lax.fori_loop(0, WIDE, forward, 0)

    for kh in range(3):
        c = kh * three
        for n in range(3):
            lanes = slice(c + n * one, c + (n + 1) * one)
            src = slice(0, one) if n == 1 else slice(one, two)
            lhs = gts if n == 0 else gt
            total = dot(lhs[0], x[kh, :, src], NN)
            for t in range(1, WIDE):
                total += dot(lhs[t], x[2 * t + kh, :, src], NN)
            g[:, lanes] = total

    def centre(b, carry):
        block = g[own_rows(b)]
        g[own_rows(b)] = block - jnp.mean(block, axis=1, keepdims=True)
        return carry

    lax.fori_loop(0, tall, centre, 0)

    def up_copy(b):
        return rc(up_out.at[own_rows(b)], up_in.at[own_rows(b)], gu_send.at[b], gu_recv.at[b], below)

    def dn_copy(b):
        return rc(dn_out.at[own_rows(b)], dn_in.at[own_rows(b)], gd_send.at[b], gd_recv.at[b], above)

    for s in range(tall - 1):
        b = tall - 1 - s

        @pl.when(r == 0)
        def _():
            up_out[own_rows(b)] = g[own_rows(b)].astype(BF)
            up_copy(b).start()

        @pl.when(r == tall - 1)
        def _():
            dn_out[own_rows(s)] = g[own_rows(s)].astype(BF)
            dn_copy(s).start()

    def relay(s):
        b = tall - 1 - s

        @pl.when((r > 0) & (b > r))
        def _():
            wait_in(up_in.at[own_rows(b)], gu_recv.at[b])
            up_out[own_rows(b)] = (g[own_rows(b)] + up_in[own_rows(b)].astype(F32)).astype(BF)
            up_copy(b).start()

        @pl.when((r < tall - 1) & (s < r))
        def _():
            wait_in(dn_in.at[own_rows(s)], gd_recv.at[s])
            dn_out[own_rows(s)] = (g[own_rows(s)] + dn_in[own_rows(s)].astype(F32)).astype(BF)
            dn_copy(s).start()

    def taps(t, kh):
        c = kh * three
        even = dot(gy[t], w[:, c + one : c + two], NN)
        odd = dot(gy[t], w[:, c + two : c + three], NN)
        odd += dot(gys[t], w[:, c : c + one], NN)
        return even, odd

    def tile_row(t, row):
        if row == 0:
            return taps(t, 1)
        even, odd = taps(t, 2)
        more_even, more_odd = taps(t + 1, 0)
        return even + more_even, odd + more_odd

    halves = (slice(0, one), slice(one, two))
    rim_pc = rc(rim_s, rim_p, e_send, e_recv.at[0], p)
    rim_qc = rc(rim_s, rim_q, e_send, e_recv.at[1], q)
    rim_zc = rc(rim_s, rim_z, e_send, e_recv.at[2], above)

    @pl.when(r > 0)
    def _():
        edge = taps(0, 0)
        for part, lanes in zip(edge, halves):
            acc[0, :, lanes] = part

        @pl.when(f % 2 == 0)
        def _():
            rim_s[...] = acc[0].astype(BF)
            rim_pc.start()

    def p_copy(k):
        return rc(to_p.at[k], from_p.at[k], d_send.at[k], d_recv.at[k], p)

    for k in (1, 0):
        t = fd if k else fp
        for row in range(2):
            for part, lanes in zip(tile_row(t, row), halves):
                to_p[k, row, :, lanes] = part.astype(BF)
        p_copy(k).start()

    @pl.when((r > 0) & (f == 1))
    def _():
        wait_in(rim_p, e_recv.at[0])
        rim_s[...] = (acc[0] + rim_p[...].astype(F32)).astype(BF)
        rim_qc.start()

    @pl.when((r > 0) & (f == 3))
    def _():
        wait_in(rim_p, e_recv.at[0])
        wait_in(rim_q, e_recv.at[1])
        rim_s[...] = (acc[0] + rim_p[...].astype(F32) + rim_q[...].astype(F32)).astype(BF)
        rim_zc.start()

    q_copy = rc(to_q, from_q, d_send.at[2], d_recv.at[2], q)
    wait_in(from_p.at[1], d_recv.at[1])
    for row in range(2):
        for part, lanes in zip(tile_row(fq, row), halves):
            to_q[row, :, lanes] = (part + from_p[1, row, :, lanes].astype(F32)).astype(BF)
    q_copy.start()
    for row in range(2):
        for part, lanes in zip(tile_row(f, row), halves):
            acc[row, :, lanes] = part
    for s in range(tall - 1):
        relay(s)

    wait_in(from_p.at[0], d_recv.at[0])
    wait_in(from_q, d_recv.at[2])
    for row in range(2):
        acc[row] += from_p[0, row].astype(F32) + from_q[row].astype(F32)

    @pl.when((r < tall - 1) & (f == 3))
    def _():
        wait_in(rim_z, e_recv.at[2])
        acc[1] += rim_z[...].astype(F32)

    for row in range(2):
        dout[row] = acc[row].astype(BF)

    gout[...] = g[own_rows(r)]

    @pl.when(r > 0)
    def _():
        wait_in(up_in.at[own_rows(r)], gu_recv.at[r])
        gout[...] += up_in[own_rows(r)].astype(F32)

    @pl.when(r < tall - 1)
    def _():
        wait_in(dn_in.at[own_rows(r)], gd_recv.at[r])
        gout[...] += dn_in[own_rows(r)].astype(F32)

    for row in range(2):
        img_copy(row, 0, p).wait_send()
        img_copy(row, 1, q).wait_send()
        fwd_copy(row).wait_send()
    tgt_copy(0, fp, p).wait_send()
    tgt_copy(1, fq, q).wait_send()
    tgt_copy(2, fd, d).wait_send()
    p_copy(0).wait_send()
    p_copy(1).wait_send()
    q_copy.wait_send()

    @pl.when((f == 3) & (r < tall - 1))
    def _():
        rim_in.wait_send()

    @pl.when((r > 0) & (f == 3))
    def _():
        rim_to_q.wait_send()

    @pl.when((r > 0) & (f % 2 == 1))
    def _():
        rim_to_p.wait_send()

    @pl.when(r > 0)
    def _():
        rim_pc.wait_send()

    for b in range(tall):
        @pl.when((r < tall - 1) & (b <= r))
        def _():
            w_copy(b, False, w_up, below).wait_send()

        @pl.when((r > 0) & (b >= r))
        def _():
            w_copy(b, False, w_dn, above).wait_send()

        @pl.when(b > r)
        def _():
            up_copy(b).wait_send()

        @pl.when(b < r)
        def _():
            dn_copy(b).wait_send()


def shards(images, target, raw_filters):
    count_img, two_rows, in_cols, cin = images.shape
    half = in_cols // 2
    own = raw_filters.shape[0]
    tall = lax.axis_size("space") // WIDE
    fan = 9 * cin
    px = count_img * half
    filters = tall * own
    own_hat, own_spread = standardize(raw_filters.reshape(own, fan))
    pair = images.reshape(count_img, two_rows, half, 2 * cin).transpose(1, 0, 2, 3)
    pair = pair.reshape(two_rows, px, 2 * cin)
    goal = target.reshape(px, tall, WIDE, own).transpose(2, 0, 1, 3).reshape(WIDE, px, filters)
    vm = pltpu.VMEM
    dma = pltpu.SemaphoreType.DMA
    row = (px, 2 * cin)
    scratch = [
        vm((2 * WIDE + 1,) + row, BF), vm((filters, fan), BF), vm((WIDE, px, filters), BF),
        vm((WIDE + 1, px, filters), BF), vm((WIDE + 1, px, filters), BF),
        vm((WIDE, filters, px), BF), vm((WIDE, filters, px), BF), vm((filters, fan), F32),
        vm((filters, fan), BF), vm((filters, fan), BF), vm((filters, fan), BF), vm((filters, fan), BF),
        vm((2, 2) + row, BF), vm((2, 2) + row, BF), vm((2,) + row, BF), vm((2,) + row, BF),
        vm((2,) + row, F32), vm(row, BF), vm(row, BF), vm(row, BF), vm(row, BF),
        dma((WIDE, 2)), dma((3, 2)), dma((tall,)), dma((tall,)), dma((tall,)),
        dma((WIDE,)), dma((3,)), dma, dma((3,)),
        dma((tall,)), dma((tall,)), dma((tall,)), dma((tall,)), dma((3,)), dma((3,)), dma((3,)), dma,
    ]
    inner, summed = pl.pallas_call(
        functools.partial(kernel, tall, own, half, cin),
        out_shape=(
            jax.ShapeDtypeStruct((2,) + row, BF),
            jax.ShapeDtypeStruct((own, fan), F32),
        ),
        in_specs=[pl.BlockSpec(memory_space=pltpu.VMEM)] * 3,
        out_specs=[pl.BlockSpec(memory_space=pltpu.VMEM)] * 2,
        scratch_shapes=scratch,
        compiler_params=pltpu.CompilerParams(
            collective_id=0, has_side_effects=True, vmem_limit_bytes=60 * 1024 * 1024
        ),
        name="tiles",
    )(pair, goal, own_hat.astype(BF))
    input_grads = inner.reshape(2, count_img, half, 2 * cin).transpose(1, 0, 2, 3).reshape(images.shape)
    first_mean = jnp.mean(summed, axis=1, keepdims=True)
    second_mean = jnp.mean(summed * own_hat, axis=1, keepdims=True)
    filter_grads = ((summed - first_mean - own_hat * second_mean) / own_spread).reshape(
        raw_filters.shape
    )
    return (input_grads, filter_grads)


def solution(mesh):
    return jax.shard_map(
        shards,
        mesh=mesh,
        in_specs=(
            P("parts", "space", None, None),
            P("parts", "space", None, None),
            P(("parts", "space"), None, None, None),
        ),
        out_specs=(P("parts", "space", None, None), P(("parts", "space"), None, None, None)),
        check_vma=False,
    )
```

time: 318 us -> 129 us (0.41)
  waiting for transfers between devices: 206 us -> 0 us
  Pallas kernels: 0 us -> 113 us
  local copies, waits for them, and re-layouts: 61.2 us -> 10.7 us
  matrix products: 23 us -> 0 us
  between operations: 14.4 us -> 0.76 us
  other arithmetic: 8.92 us -> 4.42 us
  starting transfers between devices: 3.98 us -> 0 us
    reduce_scatter x1 -> x0, waiting for transfers between devices: 158 us -> none  [shards(): lax.psum_scatter(lax.dot_general(grad_all, patches, (((0,), (0,)), ((), (...]
    pallas_call x0 -> x1, Pallas kernels: none -> 113 us  [shards(): pl.pallas_call(functools.partial(kernel, tall, own, half, cin), out_shape...]
    all_gather x1 -> x0, waiting for transfers between devices: 46.2 us -> none  [shards(): rows_bf = lax.all_gather(sent_rows, 'space', axis=0, tiled=True)]
    slice x18 -> x0, local copies, waits for them, and re-layouts: 27.9 us -> none  [the longest x9 23.7 us: shards(): tap_list.append(padded[:, kh, kw:kw + 2 * out_cols:2, :])]
    dot_general x3 -> x0, matrix products: 23 us -> none  [the longest x1 8.63 us: shards(): columns = jnp.dot(grad_block, rows_bf, preferred_element_type=jnp.float32)]
    unnamed x28 -> x9, local copies, waits for them, and re-layouts: 12.7 us -> 1.95 us
    squeeze x1 -> x0, local copies, waits for them, and re-layouts: 5.44 us -> none  [shards(): middle = place_row(grid[:, :, 1])]
    ppermute x2 -> x0, starting transfers between devices: 3.9 us -> none  [passed_along(): return lax.ppermute(block, axis, route)]
  transfers between devices with their start and end apart: 4 -> 0, of which waited for: 3 -> 0; matrix products, arithmetic and copies ran while one was open for 20% -> 0% of each run, Pallas kernels for 0% -> 0%
where the time goes in v2:
time: 129 us
  Pallas kernels  113 us (88%)
  local copies, waits for them, and re-layouts  10.7 us (8%)
  other arithmetic  4.42 us (3%)
    pallas_call x1, Pallas kernels, shards(): pl.pallas_call(functools.partial(kernel, tall, own, half, cin), out_shape...  113 us

profile of v2, /device:TPU:0, one launch (start us, length us, event | category | flops | bytes accessed | tf_op | source)
XLA Modules:
  0.0 129.1 jit_solution(17189767633114404400)
XLA Ops:
  0.6 0.0 copy-start.2
  0.6 1.3 %convert_reduce_fusion = f32[64]{0:T(128)S(1)} fusion(bf16[64,3,3,512]{3,0,2,1:T(8,128)(2,1)} %param.5), kind=kLoop, calls=%fused_computation.4 | loop fusion | flops 589760 | bytes 590080 | tf_op jit(solution)/shard_map/reduce_sum | solution.py:21
  2.0 1.4 %multiply_reduce_fusion.1 = f32[64]{0:T(128)S(1)} fusion(bf16[64,3,3,512]{3,0,2,1:T(8,128)(2,1)} %param.5, f32[64]{0:T(128)S(1)} %broadcast_multiply_fusion.2), kind=kLoop, calls=%fused_computation.2 | loop fusion | flops 1179584 | bytes 590336 | tf_op jit(solution)/shard_map/reduce_sum | solution.py:23
  3.4 0.0 copy-done.2
  3.4 0.4 reshape.53
  3.8 0.0 copy-start.3
  3.8 1.1 copy.10
  4.9 0.0 copy-done.3
  4.9 0.7 reshape.55
  5.6 0.0 copy-start
  5.6 0.8 copy.11
  6.4 1.0 copy.13.goal
  7.4 0.0 copy-done
  7.4 0.5 copy.12
  7.9 0.9 reshape.60
  8.8 1.0 fusion.hat
  9.8 113.2 %tiles.1 = (bf16[2,256,1024]{2,1,0:T(8,128)(2,1)}, f32[64,4608]{1,0:T(8,128)}) custom-call(bf16[2,256,1024]{2,1,0:T(8,128)(2,1)} %bitcast.17, bf16[4,256,256]{2,1,0:T(8,128)(2,1)} %copy.13.goal, bf16[64,4608]{1,0:T(8,128)(2,1)} %fusion.hat), custom_call_target="tpu_custom_call" | custom-call | tf_op jit(solution)/shard_map/tiles/pallas_call | solution.py:418
  123.1 1.4 %reshape.61 = bf16[4,2,128,512]{3,2,0,1:T(8,128)(2,1)S(1)} reshape(bf16[4,2,64,1024]{3,2,0,1:T(8,128)(2,1)} %bitcast.19) | data formatting | bytes 2097152 | tf_op jit(solution)/shard_map/reshape | solution.py:432
  124.5 0.0 copy-start.1
  124.5 1.1 copy.16
  125.6 0.6 copy-done.1
  126.2 0.4 fusion.1
  126.5 0.3 subtract_divide_fusion
  126.9 0.9 reshape.59
  127.8 1.4 %copy.15 = f32[64,3,3,512]{3,0,2,1:T(8,128)} copy(f32[64,3,3,512]{3,2,1,0:T(4,128)S(1)} %reshape.59) | data formatting | bytes 2359296
  (3 shorter events, 0.0 us)
Async XLA Ops:
  0.6 2.8 %copy-start.2 = (bf16[4,2,128,512]{3,2,1,0:T(8,128)(2,1)S(1)}, bf16[4,2,128,512]{3,2,1,0:T(8,128)(2,1)}, u32[]{:S(2)}) copy-start(bf16[4,2,128,512]{3,2,1,0:T(8,128)(2,1)} %param.3) | copy-start | bytes 3145732
  3.8 1.1 copy-start.3
  5.6 1.8 %copy-start = (bf16[64,3,3,512]{3,0,2,1:T(8,128)(2,1)S(1)}, bf16[64,3,3,512]{3,0,2,1:T(8,128)(2,1)}, u32[]{:S(2)}) copy-start(bf16[64,3,3,512]{3,0,2,1:T(8,128)(2,1)} %param.5) | copy-start | bytes 1769476
  124.5 1.6 %copy-start.1 = (f32[64,4608]{1,0:T(8,128)S(1)}, f32[64,4608]{1,0:T(8,128)}, u32[]{:S(2)}) copy-start(f32[64,4608]{1,0:T(8,128)} %get-tuple-element.5) | copy-start | bytes 3538948

commit v3 on v2

--- a/solution.py
+++ b/solution.py
@@ -45,7 +45,8 @@
     fd = fp + 2 - 4 * (fp // 2)
     p, q, d = base + fp, base + fq, base + fd
     above, below = me - WIDE, me + WIDE
-    px = pair.shape[1]
+    imgs = pair.shape[0]
+    px = imgs * half
     two, one = 2 * cin, cin
     three = 3 * cin
 
@@ -89,7 +90,7 @@
 
     def img_copy(row, k, to):
         slot = x.at[1 + 2 * f + row]
-        return rc(pair.at[row], slot, x_send.at[k, row], x_recv.at[f, row], to)
+        return rc(pair.at[:, row], slot, x_send.at[k, row], x_recv.at[f, row], to)
 
     def fwd_copy(row):
         slot = x.at[1 + 2 * fq + row]
@@ -102,7 +103,7 @@
         slot = w.at[own_rows(b)]
         return rc(hat if first else slot, slot, sem.at[b], w_recv.at[b], to)
 
-    rim_in = rc(pair.at[1], x.at[0], r_send.at[0], r_recv, below)
+    rim_in = rc(pair.at[:, 1], x.at[0], r_send.at[0], r_recv, below)
     rim_to_p = rc(x.at[0], x.at[0], r_send.at[1], r_recv, p)
     rim_to_q = rc(x.at[0], x.at[0], r_send.at[2], r_recv, q)
 
@@ -140,7 +141,7 @@
     tgt_copy(1, fq, q).start()
     tgt_copy(2, fd, d).start()
     for row in range(2):
-        x[1 + 2 * f + row] = pair[row]
+        x[1 + 2 * f + row] = pair[:, row]
     w[own_rows(r)] = hat[...]
     tg[f] = goal[f]
 
@@ -163,9 +164,9 @@
 
         @pl.when(r == 0)
         def _():
-            x[0] = jnp.zeros((px, two), BF)
-
-    for s in range(1, tall):
+            x[0] = jnp.zeros((imgs, half, two), BF)
+
+    for s in range(1, tall - 1):
         filters_step(s)
         if s == 1:
             forward_row(0)
@@ -179,80 +180,121 @@
         wait_in(tg.at[t], t_recv.at[t])
 
     filters = tall * own
-    place = lax.broadcasted_iota(jnp.int32, (px, filters), 0) % half
+    hf, mid = filters // 2, tall // 2
+    own_half = r // mid
+    place = lax.broadcasted_iota(jnp.int32, (px, hf), 0) % half
     gy[WIDE] = jnp.zeros((px, filters), BF)
     gys[WIDE] = jnp.zeros((px, filters), BF)
 
-    def forward(t, carry):
-        both = jnp.zeros((px, filters), F32)
-        left = jnp.zeros((px, filters), F32)
+    def img(index, lanes):
+        return x[index, :, :, lanes].reshape(px, lanes.stop - lanes.start)
+
+    def forward(h, t):
+        part = pl.ds(pl.multiple_of(h * hf, hf), hf)
+        both = jnp.zeros((px, hf), F32)
+        left = jnp.zeros((px, hf), F32)
         for kh in range(3):
             c = kh * three
-            both += dot(x[2 * t + kh], w[:, c + one : c + three], NT)
-            left += dot(x[2 * t + kh, :, one:two], w[:, c : c + one], NT)
+            both += dot(img(2 * t + kh, slice(0, two)), w[part, c + one : c + three], NT)
+            left += dot(img(2 * t + kh, slice(one, two)), w[part, c : c + one], NT)
         out = both + jnp.where(place == 0, 0.0, pltpu.roll(left, 1, 0))
-        grad = ((out - tg[t].astype(F32)) * GRAD_SCALE).astype(BF)
+        grad = ((out - tg[t, :, part].astype(F32)) * GRAD_SCALE).astype(BF)
         wide = grad.astype(F32)
         ahead = jnp.where(place == half - 1, 0.0, pltpu.roll(wide, px - 1, 0))
-        gy[t] = grad
-        gys[t] = ahead.astype(BF)
-        gt[t] = wide.T.astype(BF)
-        gts[t] = ahead.T.astype(BF)
-        return carry
-
-    lax.fori_loop(0, WIDE, forward, 0)
-
-    for kh in range(3):
-        c = kh * three
-        for n in range(3):
-            lanes = slice(c + n * one, c + (n + 1) * one)
-            src = slice(0, one) if n == 1 else slice(one, two)
-            lhs = gts if n == 0 else gt
-            total = dot(lhs[0], x[kh, :, src], NN)
-            for t in range(1, WIDE):
-                total += dot(lhs[t], x[2 * t + kh, :, src], NN)
-            g[:, lanes] = total
-
-    def centre(b, carry):
-        block = g[own_rows(b)]
-        g[own_rows(b)] = block - jnp.mean(block, axis=1, keepdims=True)
-        return carry
-
-    lax.fori_loop(0, tall, centre, 0)
-
-    def up_copy(b):
-        return rc(up_out.at[own_rows(b)], up_in.at[own_rows(b)], gu_send.at[b], gu_recv.at[b], below)
-
-    def dn_copy(b):
-        return rc(dn_out.at[own_rows(b)], dn_in.at[own_rows(b)], gd_send.at[b], gd_recv.at[b], above)
-
-    for s in range(tall - 1):
-        b = tall - 1 - s
+        gy[t, :, part] = grad
+        gys[t, :, part] = ahead.astype(BF)
+        gt[t, part] = wide.T.astype(BF)
+        gts[t, part] = ahead.T.astype(BF)
+
+    def filter_terms(h):
+        part = pl.ds(pl.multiple_of(h * hf, hf), hf)
+        for kh in range(3):
+            c = kh * three
+            for n in range(3):
+                lanes = slice(c + n * one, c + (n + 1) * one)
+                src = slice(0, one) if n == 1 else slice(one, two)
+                lhs = gts if n == 0 else gt
+                total = dot(lhs[0, part], img(kh, src), NN)
+                for t in range(1, WIDE):
+                    total += dot(lhs[t, part], img(2 * t + kh, src), NN)
+                g[part, lanes] = total
+
+        def centre(i, carry):
+            rows = own_rows(h * mid + i)
+            block = g[rows]
+            g[rows] = block - jnp.mean(block, axis=1, keepdims=True)
+            return carry
+
+        lax.fori_loop(0, mid, centre, 0)
+
+    fan = w.shape[1]
+    cols = (slice(0, fan // 2), slice(fan // 2, fan))
+
+    def up_copy(b, k):
+        at = (own_rows(b), cols[k])
+        return rc(up_out.at[at], up_in.at[at], gu_send.at[b, k], gu_recv.at[b, k], below)
+
+    def dn_copy(b, k):
+        at = (own_rows(b), cols[k])
+        return rc(dn_out.at[at], dn_in.at[at], gd_send.at[b, k], gd_recv.at[b, k], above)
+
+    def first_up(b):
+        for k in range(2):
+            at = (own_rows(b), cols[k])
+            up_out[at] = g[at].astype(BF)
+            up_copy(b, k).start()
+
+    def first_dn(b):
+        for k in range(2):
+            at = (own_rows(b), cols[k])
+            dn_out[at] = g[at].astype(BF)
+            dn_copy(b, k).start()
+
+    for turn in range(2):
+        if turn == 1:
+            filters_step(tall - 1)
+        h = own_half if turn == 0 else 1 - own_half
+
+        def step(t, carry):
+            forward(h, t)
+            return carry
+
+        lax.fori_loop(0, WIDE, step, 0)
+        filter_terms(h)
 
         @pl.when(r == 0)
         def _():
-            up_out[own_rows(b)] = g[own_rows(b)].astype(BF)
-            up_copy(b).start()
+            for i in range(mid):
+                b = turn * mid + mid - 1 - i
+                if b > 0:
+                    first_up(b)
 
         @pl.when(r == tall - 1)
         def _():
-            dn_out[own_rows(s)] = g[own_rows(s)].astype(BF)
-            dn_copy(s).start()
-
-    def relay(s):
-        b = tall - 1 - s
-
-        @pl.when((r > 0) & (b > r))
-        def _():
-            wait_in(up_in.at[own_rows(b)], gu_recv.at[b])
-            up_out[own_rows(b)] = (g[own_rows(b)] + up_in[own_rows(b)].astype(F32)).astype(BF)
-            up_copy(b).start()
-
-        @pl.when((r < tall - 1) & (s < r))
-        def _():
-            wait_in(dn_in.at[own_rows(s)], gd_recv.at[s])
-            dn_out[own_rows(s)] = (g[own_rows(s)] + dn_in[own_rows(s)].astype(F32)).astype(BF)
-            dn_copy(s).start()
+            for i in range(mid):
+                b = (1 - turn) * mid + i
+                if b < tall - 1:
+                    first_dn(b)
+
+    def relay(step):
+        b_up = tall - 1 - (step - r)
+        b_dn = step - (tall - 1 - r)
+
+        @pl.when((r > 0) & (b_up <= tall - 1) & (b_up > r))
+        def _():
+            for k in range(2):
+                at = (own_rows(b_up), cols[k])
+                wait_in(up_in.at[at], gu_recv.at[b_up, k])
+                up_out[at] = (g[at] + up_in[at].astype(F32)).astype(BF)
+                up_copy(b_up, k).start()
+
+        @pl.when((r < tall - 1) & (b_dn >= 0) & (b_dn < r))
+        def _():
+            for k in range(2):
+                at = (own_rows(b_dn), cols[k])
+                wait_in(dn_in.at[at], gd_recv.at[b_dn, k])
+                dn_out[at] = (g[at] + dn_in[at].astype(F32)).astype(BF)
+                dn_copy(b_dn, k).start()
 
     def taps(t, kh):
         c = kh * three
@@ -307,17 +349,18 @@
         rim_s[...] = (acc[0] + rim_p[...].astype(F32) + rim_q[...].astype(F32)).astype(BF)
         rim_zc.start()
 
+    relay(1)
     q_copy = rc(to_q, from_q, d_send.at[2], d_recv.at[2], q)
     wait_in(from_p.at[1], d_recv.at[1])
     for row in range(2):
         for part, lanes in zip(tile_row(fq, row), halves):
             to_q[row, :, lanes] = (part + from_p[1, row, :, lanes].astype(F32)).astype(BF)
     q_copy.start()
+    for step in range(2, tall - 1):
+        relay(step)
     for row in range(2):
         for part, lanes in zip(tile_row(f, row), halves):
             acc[row, :, lanes] = part
-    for s in range(tall - 1):
-        relay(s)
 
     wait_in(from_p.at[0], d_recv.at[0])
     wait_in(from_q, d_recv.at[2])
@@ -330,18 +373,20 @@
         acc[1] += rim_z[...].astype(F32)
 
     for row in range(2):
-        dout[row] = acc[row].astype(BF)
+        dout[:, row] = acc[row].astype(BF).reshape(imgs, half, two)
 
     gout[...] = g[own_rows(r)]
 
     @pl.when(r > 0)
     def _():
-        wait_in(up_in.at[own_rows(r)], gu_recv.at[r])
+        for k in range(2):
+            wait_in(up_in.at[own_rows(r), cols[k]], gu_recv.at[r, k])
         gout[...] += up_in[own_rows(r)].astype(F32)
 
     @pl.when(r < tall - 1)
     def _():
-        wait_in(dn_in.at[own_rows(r)], gd_recv.at[r])
+        for k in range(2):
+            wait_in(dn_in.at[own_rows(r), cols[k]], gd_recv.at[r, k])
         gout[...] += dn_in[own_rows(r)].astype(F32)
 
     for row in range(2):
@@ -382,11 +427,13 @@
 
         @pl.when(b > r)
         def _():
-            up_copy(b).wait_send()
+            up_copy(b, 0).wait_send()
+            up_copy(b, 1).wait_send()
 
         @pl.when(b < r)
         def _():
-            dn_copy(b).wait_send()
+            dn_copy(b, 0).wait_send()
+            dn_copy(b, 1).wait_send()
 
 
 def shards(images, target, raw_filters):
@@ -398,14 +445,13 @@
     px = count_img * half
     filters = tall * own
     own_hat, own_spread = standardize(raw_filters.reshape(own, fan))
-    pair = images.reshape(count_img, two_rows, half, 2 * cin).transpose(1, 0, 2, 3)
-    pair = pair.reshape(two_rows, px, 2 * cin)
+    pair = images.reshape(count_img, two_rows, half, 2 * cin)
     goal = target.reshape(px, tall, WIDE, own).transpose(2, 0, 1, 3).reshape(WIDE, px, filters)
     vm = pltpu.VMEM
     dma = pltpu.SemaphoreType.DMA
     row = (px, 2 * cin)
     scratch = [
-        vm((2 * WIDE + 1,) + row, BF), vm((filters, fan), BF), vm((WIDE, px, filters), BF),
+        vm((2 * WIDE + 1, count_img, half, 2 * cin), BF), vm((filters, fan), BF), vm((WIDE, px, filters), BF),
         vm((WIDE + 1, px, filters), BF), vm((WIDE + 1, px, filters), BF),
         vm((WIDE, filters, px), BF), vm((WIDE, filters, px), BF), vm((filters, fan), F32),
         vm((filters, fan), BF), vm((filters, fan), BF), vm((filters, fan), BF), vm((filters, fan), BF),
@@ -413,12 +459,12 @@
         vm((2,) + row, F32), vm(row, BF), vm(row, BF), vm(row, BF), vm(row, BF),
         dma((WIDE, 2)), dma((3, 2)), dma((tall,)), dma((tall,)), dma((tall,)),
         dma((WIDE,)), dma((3,)), dma, dma((3,)),
-        dma((tall,)), dma((tall,)), dma((tall,)), dma((tall,)), dma((3,)), dma((3,)), dma((3,)), dma,
+        dma((tall, 2)), dma((tall, 2)), dma((tall, 2)), dma((tall, 2)), dma((3,)), dma((3,)), dma((3,)), dma,
     ]
     inner, summed = pl.pallas_call(
         functools.partial(kernel, tall, own, half, cin),
         out_shape=(
-            jax.ShapeDtypeStruct((2,) + row, BF),
+            jax.ShapeDtypeStruct(pair.shape, BF),
             jax.ShapeDtypeStruct((own, fan), F32),
         ),
         in_specs=[pl.BlockSpec(memory_space=pltpu.VMEM)] * 3,
@@ -429,7 +475,7 @@
         ),
         name="tiles",
     )(pair, goal, own_hat.astype(BF))
-    input_grads = inner.reshape(2, count_img, half, 2 * cin).transpose(1, 0, 2, 3).reshape(images.shape)
+    input_grads = inner.reshape(images.shape)
     first_mean = jnp.mean(summed, axis=1, keepdims=True)
     second_mean = jnp.mean(summed * own_hat, axis=1, keepdims=True)
     filter_grads = ((summed - first_mean - own_hat * second_mean) / own_spread).reshape(

time: 129 us -> 117 us (0.907); the launches traced: 129 us -> 115 us
  Pallas kernels: 113 us -> 99.9 us
    pallas_call x1, Pallas kernels: 113 us -> 99.9 us  [shards(): pl.pallas_call(functools.partial(kernel, tall, own, half, cin), out_shape...]
    reshape x4 -> x2, local copies, waits for them, and re-layouts: 3.98 us -> 3.47 us  [the longest x1 2.29 us: shards(): input_grads = inner.reshape(images.shape)]
where the time goes in v3:
time: 117 us; the launch traced here: 115 us
  Pallas kernels  99.9 us (85%)
  local copies, waits for them, and re-layouts  9.65 us (8%)
  other arithmetic  4.38 us (4%)
    pallas_call x1, Pallas kernels, shards(): pl.pallas_call(functools.partial(kernel, tall, own, half, cin), out_shape...  99.9 us

profile of v3, /device:TPU:0, one launch (start us, length us, event | category | flops | bytes accessed | tf_op | source)
XLA Modules:
  0.0 114.7 jit_solution(13349097453939076392)
XLA Ops:
  0.6 0.0 copy-start.2
  0.6 1.3 %convert_reduce_fusion = f32[64]{0:T(128)S(1)} fusion(bf16[64,3,3,512]{3,0,2,1:T(8,128)(2,1)} %param.5), kind=kLoop, calls=%fused_computation.4 | loop fusion | flops 589760 | bytes 590080 | tf_op jit(solution)/shard_map/reduce_sum | solution.py:21
  2.0 1.4 %multiply_reduce_fusion.1 = f32[64]{0:T(128)S(1)} fusion(bf16[64,3,3,512]{3,0,2,1:T(8,128)(2,1)} %param.5, f32[64]{0:T(128)S(1)} %broadcast_multiply_fusion.2), kind=kLoop, calls=%fused_computation.2 | loop fusion | flops 1179584 | bytes 590336 | tf_op jit(solution)/shard_map/reduce_sum | solution.py:23
  3.4 0.0 copy-start.3
  3.4 0.0 copy-done.2
  3.4 1.2 %reshape.47.pair = bf16[4,2,64,1024]{3,2,1,0:T(8,128)(2,1)} reshape(bf16[4,2,128,512]{3,2,1,0:T(8,128)(2,1)S(1)} %copy-done.2) | data formatting | bytes 2097152 | tf_op jit(solution)/shard_map/reshape | solution.py:448
  4.6 0.0 copy-done.3
  4.6 0.7 reshape.48
  5.2 0.0 copy-start
  5.3 0.8 copy.8
  6.1 1.0 copy.10.goal
  7.1 0.0 copy-done
  7.1 0.5 copy.9
  7.6 0.9 reshape.52
  8.5 1.0 fusion.hat
  9.5 99.9 %tiles.1 = (bf16[4,2,64,1024]{3,2,1,0:T(8,128)(2,1)}, f32[64,4608]{1,0:T(8,128)}) custom-call(bf16[4,2,64,1024]{3,2,1,0:T(8,128)(2,1)} %reshape.47.pair, bf16[4,256,256]{2,1,0:T(8,128)(2,1)} %copy.10.goal, bf16[64,4608]{1,0:T(8,128)(2,1)} %fusion.hat), custom_call_target="tpu_custom_call" | custom-call | tf_op jit(solution)/shard_map/tiles/pallas_call | solution.py:464
  109.4 0.0 copy-start.1
  109.4 2.3 %reshape.50 = bf16[4,2,128,512]{3,2,1,0:T(8,128)(2,1)} reshape(bf16[4,2,64,1024]{3,2,1,0:T(8,128)(2,1)} %get-tuple-element.4) | data formatting | bytes 2097152 | tf_op jit(solution)/shard_map/reshape | solution.py:478
  111.7 0.0 copy-done.1
  111.7 0.3 fusion.1
  112.1 0.3 subtract_divide_fusion
  112.4 0.9 reshape.51
  113.3 1.4 %copy.11 = f32[64,3,3,512]{3,0,2,1:T(8,128)} copy(f32[64,3,3,512]{3,2,1,0:T(4,128)S(1)} %reshape.51) | data formatting | bytes 2359296
  (3 shorter events, 0.0 us)
Async XLA Ops:
  0.6 2.8 %copy-start.2 = (bf16[4,2,128,512]{3,2,1,0:T(8,128)(2,1)S(1)}, bf16[4,2,128,512]{3,2,1,0:T(8,128)(2,1)}, u32[]{:S(2)}) copy-start(bf16[4,2,128,512]{3,2,1,0:T(8,128)(2,1)} %param.3) | copy-start | bytes 3145732
  3.4 1.2 %copy-start.3 = (bf16[4,1,64,1024]{3,2,1,0:T(8,128)(2,1)S(1)}, bf16[4,1,64,1024]{3,2,1,0:T(8,128)(2,1)}, u32[]{:S(2)}) copy-start(bf16[4,1,64,1024]{3,2,1,0:T(8,128)(2,1)} %param.4) | copy-start | bytes 1572868
  5.2 1.8 %copy-start = (bf16[64,3,3,512]{3,0,2,1:T(8,128)(2,1)S(1)}, bf16[64,3,3,512]{3,0,2,1:T(8,128)(2,1)}, u32[]{:S(2)}) copy-start(bf16[64,3,3,512]{3,0,2,1:T(8,128)(2,1)} %param.5) | copy-start | bytes 1769476
  109.4 2.3 %copy-start.1 = (f32[64,4608]{1,0:T(8,128)S(1)}, f32[64,4608]{1,0:T(8,128)}, u32[]{:S(2)}) copy-start(f32[64,4608]{1,0:T(8,128)} %get-tuple-element.5) | copy-start | bytes 3538948

commit v4 on v3

--- a/solution.py
+++ b/solution.py
@@ -128,11 +128,12 @@
             def _():
                 w_copy(b_dn, s == 0, w_dn, above).start()
 
+    filters_step(0)
+
     @pl.when((f == 3) & (r < tall - 1))
     def _():
         rim_in.start()
 
-    filters_step(0)
     for row in range(2):
         img_copy(row, 1, q).start()
     for row in range(2):

time: 117 us -> 117 us (level)
  no operation moved by 1% of the time
where the time goes in v4:
time: 117 us; the launch traced here: 115 us
  Pallas kernels  99.9 us (85%)
  local copies, waits for them, and re-layouts  9.65 us (8%)
  other arithmetic  4.38 us (4%)
    pallas_call x1, Pallas kernels, shards(): pl.pallas_call(functools.partial(kernel, tall, own, half, cin), out_shape...  99.9 us

profile of v4, /device:TPU:0, one launch (start us, length us, event | category | flops | bytes accessed | tf_op | source)
XLA Modules:
  0.0 114.7 jit_solution(7611359762423003537)
XLA Ops:
  0.6 0.0 copy-start.2
  0.6 1.3 %convert_reduce_fusion = f32[64]{0:T(128)S(1)} fusion(bf16[64,3,3,512]{3,0,2,1:T(8,128)(2,1)} %param.5), kind=kLoop, calls=%fused_computation.4 | loop fusion | flops 589760 | bytes 590080 | tf_op jit(solution)/shard_map/reduce_sum | solution.py:21
  2.0 1.4 %multiply_reduce_fusion.1 = f32[64]{0:T(128)S(1)} fusion(bf16[64,3,3,512]{3,0,2,1:T(8,128)(2,1)} %param.5, f32[64]{0:T(128)S(1)} %broadcast_multiply_fusion.2), kind=kLoop, calls=%fused_computation.2 | loop fusion | flops 1179584 | bytes 590336 | tf_op jit(solution)/shard_map/reduce_sum | solution.py:23
  3.4 0.0 copy-start.3
  3.4 0.0 copy-done.2
  3.4 1.2 %reshape.47.pair = bf16[4,2,64,1024]{3,2,1,0:T(8,128)(2,1)} reshape(bf16[4,2,128,512]{3,2,1,0:T(8,128)(2,1)S(1)} %copy-done.2) | data formatting | bytes 2097152 | tf_op jit(solution)/shard_map/reshape | solution.py:449
  4.6 0.0 copy-done.3
  4.6 0.7 reshape.48
  5.2 0.0 copy-start
  5.3 0.8 copy.8
  6.1 1.0 copy.10.goal
  7.1 0.0 copy-done
  7.1 0.5 copy.9
  7.6 0.9 reshape.52
  8.5 1.0 fusion.hat
  9.5 99.9 %tiles.1 = (bf16[4,2,64,1024]{3,2,1,0:T(8,128)(2,1)}, f32[64,4608]{1,0:T(8,128)}) custom-call(bf16[4,2,64,1024]{3,2,1,0:T(8,128)(2,1)} %reshape.47.pair, bf16[4,256,256]{2,1,0:T(8,128)(2,1)} %copy.10.goal, bf16[64,4608]{1,0:T(8,128)(2,1)} %fusion.hat), custom_call_target="tpu_custom_call" | custom-call | tf_op jit(solution)/shard_map/tiles/pallas_call | solution.py:465
  109.4 0.0 copy-start.1
  109.4 2.3 %reshape.50 = bf16[4,2,128,512]{3,2,1,0:T(8,128)(2,1)} reshape(bf16[4,2,64,1024]{3,2,1,0:T(8,128)(2,1)} %get-tuple-element.4) | data formatting | bytes 2097152 | tf_op jit(solution)/shard_map/reshape | solution.py:479
  111.7 0.0 copy-done.1
  111.7 0.3 fusion.1
  112.1 0.3 subtract_divide_fusion
  112.4 0.9 reshape.51
  113.3 1.4 %copy.11 = f32[64,3,3,512]{3,0,2,1:T(8,128)} copy(f32[64,3,3,512]{3,2,1,0:T(4,128)S(1)} %reshape.51) | data formatting | bytes 2359296
  (3 shorter events, 0.0 us)
Async XLA Ops:
  0.6 2.8 %copy-start.2 = (bf16[4,2,128,512]{3,2,1,0:T(8,128)(2,1)S(1)}, bf16[4,2,128,512]{3,2,1,0:T(8,128)(2,1)}, u32[]{:S(2)}) copy-start(bf16[4,2,128,512]{3,2,1,0:T(8,128)(2,1)} %param.3) | copy-start | bytes 3145732
  3.4 1.2 %copy-start.3 = (bf16[4,1,64,1024]{3,2,1,0:T(8,128)(2,1)S(1)}, bf16[4,1,64,1024]{3,2,1,0:T(8,128)(2,1)}, u32[]{:S(2)}) copy-start(bf16[4,1,64,1024]{3,2,1,0:T(8,128)(2,1)} %param.4) | copy-start | bytes 1572868
  5.2 1.8 %copy-start = (bf16[64,3,3,512]{3,0,2,1:T(8,128)(2,1)S(1)}, bf16[64,3,3,512]{3,0,2,1:T(8,128)(2,1)}, u32[]{:S(2)}) copy-start(bf16[64,3,3,512]{3,0,2,1:T(8,128)(2,1)} %param.5) | copy-start | bytes 1769476
  109.4 2.3 %copy-start.1 = (f32[64,4608]{1,0:T(8,128)S(1)}, f32[64,4608]{1,0:T(8,128)}, u32[]{:S(2)}) copy-start(f32[64,4608]{1,0:T(8,128)} %get-tuple-element.5) | copy-start | bytes 3538948
